TPU v7x, 32 devices: a whole 2x2x4 slice. The times are simulated.
32 devices in a mesh: row: 4 (over z), col: 8 (over y, x, core).
Axes of the slice: x: 2, y: 2, z: 4, core: 2. Of those that a mesh axis runs over, the one named last changes fastest.
Arguments:
- panel: float32 [8, 1024, 8192], P(None, 'row', 'col'), may hold values from -0.0625 to 0.0625
- prior_y: float32 [8192, 1024], P('col', 'row'), may hold values from -6 to 6
- right_side: float32 [8, 1024, 1024], P(None, 'row', 'col'), may hold values from -6 to 6
- inv_blocks: float32 [2, 1024, 1024], P(None, 'row'), may hold values from -2 to 2, as said below
- lower_block: float32 [1024, 1024], P('row'), may hold values from -0.1875 to 0.1875
Outputs:
- y_window: float32 [2, 1024, 1024], P(None, 'row', 'col')
- pending: float32 [6, 1024, 1024], P(None, 'row', 'col')
Inputs may be any that keep to these rules, and one draw needn't show every extreme that they name: `inv_blocks`: each block is lower triangular with a positive diagonal.
All inputs are finite; a program needn't handle non-finite values.
Results may differ from a plain program's by a relative error of at most 0.000073.
Values sent between devices are 32-bit elements; how exact they have to be, the bound alone decides.
A program may use at most 64 MiB of HBM per device.

v0:
```python
import jax
import jax.numpy as jnp
from jax import lax
from jax.sharding import PartitionSpec as P


def body(panel, prior_y, right_side, inv_blocks, lower_block):
    highest = lax.Precision.HIGHEST
    terms = jnp.einsum(
        "sip,pm->sim",
        panel,
        lax.all_gather(prior_y, "row", axis=1, tiled=True),
        precision=highest,
        preferred_element_type=jnp.float32,
    )
    panel_total = lax.psum_scatter(terms, "col", scatter_dimension=2, tiled=True)
    residual = right_side - panel_total
    first_all_rows = lax.all_gather(residual[0], "row", axis=0, tiled=True)
    first_solution = jnp.dot(
        inv_blocks[0], first_all_rows, precision=highest, preferred_element_type=jnp.float32
    )
    solved_all = lax.all_gather(first_solution, "row", axis=0, tiled=True)
    second_residual = residual[1] - jnp.dot(
        lower_block, solved_all, precision=highest, preferred_element_type=jnp.float32
    )
    second_all_rows = lax.all_gather(second_residual, "row", axis=0, tiled=True)
    second_solution = jnp.dot(
        inv_blocks[1], second_all_rows, precision=highest, preferred_element_type=jnp.float32
    )
    return (jnp.stack([first_solution, second_solution]), residual[2:])


def solution(mesh):
    placed = (
        P(None, "row", "col"),
        P("col", "row"),
        P(None, "row", "col"),
        P(None, "row", None),
        P("row", None),
    )
    return jax.shard_map(
        body,
        mesh=mesh,
        in_specs=placed,
        out_specs=(P(None, "row", "col"), P(None, "row", "col")),
        check_vma=False,
    )
```

profile of v0, /device:TPU:0, one launch (start us, length us, event | category | flops | bytes accessed | tf_op | source)
XLA Modules:
  0.0 256.4 jit_solution(16269681852053986856)
XLA Ops:
  7.2 0.0 copy-start
  7.2 0.0 all-gather.3.cloned.1.call-start
  7.2 0.7 all-gather.3.cloned.1.call-update
  7.9 0.0 reduce-scatter.2.cloned.1.call-start
  8.0 85.1 %all-gather.3.cloned.1.call-done = f32[1024,1024]{1,0:T(8,128)} async-done(((f32[1024,256]{1,0:T(8,128)}), f32[1024,1024]{1,0:T(8,128)}) %all-gather.3.cloned.1.call-update) | async-done | bytes 4194320 | tf_op jit(solution)/shard_map/all_gather | solution.py:12
  93.1 32.5 %fusion = f32[8,256,1024]{2,1,0:T(8,128)} fusion(f32[8,256,1024]{2,1,0:T(8,128)} %param.5, f32[1024,1024]{1,0:T(8,128)} %all-gather.3.cloned.1.call-done), kind=kOutput, calls=%fused_computation | convolution fusion | flops 25769803776 | bytes 20971520 | tf_op jit(solution)/shard_map/sip,pm->sim/dot_general | solution.py:9
  125.6 0.0 reduce-scatter.2.cloned.1.call-update
  125.6 0.0 copy-start.1
  125.6 69.9 %reduce-scatter.2.cloned.1.call-done = f32[8,256,128]{2,1,0:T(8,128)} async-done(((f32[8,256,1024]{2,1,0:T(8,128)}), f32[8,256,128]{2,1,0:T(8,128)}) %reduce-scatter.2.cloned.1.call-update) | async-done | bytes 1048592 | tf_op jit(solution)/shard_map/reduce_scatter | solution.py:16
  195.6 1.6 sub.6
  197.2 0.9 slice.22
  198.2 15.6 %all-gather = f32[1,1024,128]{2,1,0:T(8,128)S(1)} all-gather(f32[1,256,128]{2,1,0:T(8,128)S(1)} %slice.20), channel_id=2, replica_groups=mesh['row'=4,'col'=8] {'row'}, dimensions={1}, use_global_device_ids=true | all-gather | bytes 655360 | tf_op jit(solution)/shard_map/all_gather | solution.py:18
  213.8 0.0 copy-done.1
  213.8 1.0 fusion.4
  214.8 16.3 %all_gather.14 = f32[1024,128]{0,1:T(8,128)S(1)} all-gather(f32[256,128]{0,1:T(8,128)S(1)} %bitcast.31), channel_id=1, replica_groups=mesh['row'=4,'col'=8] {'row'}, dimensions={0}, use_global_device_ids=true | all-gather | bytes 655360 | tf_op jit(solution)/shard_map/all_gather | solution.py:22
  231.1 0.0 copy-done
  231.1 1.0 fusion.2
  232.1 15.5 %all_gather.15 = f32[1024,128]{1,0:T(8,128)S(1)} all-gather(f32[256,128]{1,0:T(8,128)S(1)} %fusion.2), channel_id=1, replica_groups=mesh['row'=4,'col'=8] {'row'}, dimensions={0}, use_global_device_ids=true | all-gather | bytes 655360 | tf_op jit(solution)/shard_map/all_gather | solution.py:26
  247.7 1.0 convolution_bitcast_fusion
  248.7 0.8 copy.7
  (2 shorter events, 0.0 us)
Async XLA Ops:
  7.2 224.0 %copy-start = (f32[256,1024]{1,0:T(8,128)S(1)}, f32[256,1024]{1,0:T(8,128)}, u32[]{:S(2)}) copy-start(f32[256,1024]{1,0:T(8,128)} %param.9) | copy-start | bytes 3145732
  7.2 85.9 %all-gather.3.cloned.1.call-start = ((), (), s32[]{:S(2)}) async-start(), calls=%async_computation.1 | async-start | bytes 5242880 | tf_op jit(solution)/shard_map/all_gather | solution.py:12
  7.9 187.7 %reduce-scatter.2.cloned.1.call-start = ((), (), s32[]{:S(2)}) async-start(), calls=%async_computation.2 | async-start | bytes 9437184 | tf_op jit(solution)/shard_map/reduce_scatter | solution.py:16
  125.6 88.2 %copy-start.1 = (f32[2,256,1024]{2,1,0:T(8,128)S(1)}, f32[2,256,1024]{2,1,0:T(8,128)}, u32[]{:S(2)}) copy-start(f32[2,256,1024]{2,1,0:T(8,128)} %param.8) | copy-start | bytes 6291460
Sparse Core Ops, SparseCore 0:
  9.6 83.4 all-gather.2
  125.7 69.7 reduce-scatter.1
where the time goes:
time: 257 us; the launch traced here: 256 us
  waiting for transfers between devices  156 us (61%)
  blocking collectives  47.5 us (18%)
  matrix products  35.5 us (14%)
  between operations  14.1 us (5%)
    all_gather x1, waiting for transfers between devices, body(): lax.all_gather(prior_y, 'row', axis=1, tiled=True)  85.1 us
    reduce_scatter x1, waiting for transfers between devices, body(): lax.psum_scatter(terms, 'col', scatter_dimension=2, tiled=True)  69.9 us
    dot_general x1, matrix products, body(): jnp.einsum('sip,pm->sim', panel, lax.all_gather(prior_y, 'row', axis=1, t...  32.5 us
    all_gather x1, blocking collectives, body(): solved_all = lax.all_gather(first_solution, 'row', axis=0, tiled=True)  16.3 us
    all_gather x1, blocking collectives, body(): first_all_rows = lax.all_gather(residual[0], 'row', axis=0, tiled=True)  15.6 us
    all_gather x1, blocking collectives, body(): second_all_rows = lax.all_gather(second_residual, 'row', axis=0, tiled=True)  15.5 us
  transfers between devices with their start and end apart: 2, of which 2 were waited for; matrix products, arithmetic and copies ran while one was open for 0% of the time, Pallas kernels for 0%

commit v1 on v0

--- a/solution.py
+++ b/solution.py
@@ -1,10 +1,348 @@
+import functools
+
 import jax
 import jax.numpy as jnp
 from jax import lax
+from jax.experimental import pallas as pl
+from jax.experimental.pallas import tpu as pltpu
 from jax.sharding import PartitionSpec as P
 
-
-def body(panel, prior_y, right_side, inv_blocks, lower_block):
+MESH = pl.DeviceIdType.MESH
+F32 = jnp.float32
+BF16 = jnp.bfloat16
+
+
+def split(x):
+    high = x.astype(BF16)
+    return high, (x - high.astype(F32)).astype(BF16)
+
+
+def dot3(a, b):
+    a_hi, a_lo = a
+    b_hi, b_lo = b
+    dot = functools.partial(jnp.dot, preferred_element_type=F32)
+    return dot(a_hi, b_hi) + (dot(a_hi, b_lo) + dot(a_lo, b_hi))
+
+
+def kernel(
+    panel, prior, right, inv, lower, y_out, pend_out,
+    pf, p_hi, p_lo, y_buf, y_hi, y_lo, core_src, core_dst, part, first_dst, second_dst,
+    rhs, inv_v, low_v, r0_all, y0_all, s1_all, r1,
+    load_sem, panel_sem, y_send, y_recv, core_send, core_recv, first_send, first_recv,
+    second_send, second_recv, chain_send, chain_recv,
+):
+    steps, rows, depth = pf.shape
+    chunks = core_send.shape[1]
+    per = steps // chunks
+    z = lax.axis_index("row")
+    col = lax.axis_index("col")
+    y, x, core = col // 4, (col // 2) % 2, col % 2
+    chip = col // 2
+    sibling = col + 1 - 2 * core
+    x_near, y_near = col + 2 - 4 * x, col + 4 - 8 * y
+    first = x_near + core * (y_near - x_near)
+    second = y_near + core * (x_near - y_near)
+    f = x + core * (y - x)
+    g = y + core * (x - y)
+    middle = (z == 1) | (z == 2)
+    upper = z // 2
+    z_fold = z + upper * (3 - 2 * z)
+
+    def block_at(k):
+        b = (z_fold, 1 - z_fold, 2, 3)[k]
+        return b + upper * (3 - 2 * b)
+
+    own = pltpu.make_async_copy(prior, y_buf.at[z], load_sem.at[0])
+    own.start()
+    panel_copies = [
+        pltpu.make_async_copy(panel.at[s], pf.at[s], panel_sem.at[s]) for s in range(steps)
+    ]
+    for copy in panel_copies:
+        copy.start()
+    loads = [
+        pltpu.make_async_copy(right, rhs, load_sem.at[1]),
+        pltpu.make_async_copy(inv, inv_v, load_sem.at[2]),
+        pltpu.make_async_copy(lower, low_v, load_sem.at[3]),
+    ]
+    for copy in loads:
+        copy.start()
+
+    barrier = pltpu.get_barrier_semaphore()
+    for partner in (sibling, x_near, y_near):
+        pl.semaphore_signal(barrier, inc=1, device_id=(z, partner), device_id_type=MESH)
+    for j in range(1, 4):
+        pl.semaphore_signal(barrier, inc=1, device_id=((z + j) % 4, col), device_id_type=MESH)
+    pl.semaphore_wait(barrier, 6)
+
+    def along_z(src, b, target, sem):
+        return pltpu.make_async_remote_copy(
+            src_ref=src, dst_ref=y_buf.at[b], send_sem=y_send.at[sem], recv_sem=y_recv.at[b],
+            device_id=(target, col), device_id_type=MESH,
+        )
+
+    def forward(b, finish=False):
+        @pl.when((b < z) & (z < 3))
+        def _():
+            copy = along_z(y_buf.at[b], b, z + 1, 2 + b)
+            copy.wait_send() if finish else copy.start()
+
+        @pl.when((b > z) & (z > 0))
+        def _():
+            copy = along_z(y_buf.at[b], b, z - 1, 2 + b)
+            copy.wait_send() if finish else copy.start()
+
+    def own_sends(finish=False):
+        @pl.when(z < 3)
+        def _():
+            copy = along_z(prior, z, z + 1, 0)
+            copy.wait_send() if finish else copy.start()
+
+        @pl.when(z > 0)
+        def _():
+            copy = along_z(prior, z, z - 1, 1)
+            copy.wait_send() if finish else copy.start()
+
+    def arrived(b):
+        along_z(y_buf.at[b], b, (z + 1) % 4, 0).wait_recv()
+
+    def piece(ref, k, c):
+        return ref.at[k, pl.ds(c * per, per)]
+
+    def core_copy(k, c):
+        return pltpu.make_async_remote_copy(
+            src_ref=piece(core_src, k, c), dst_ref=piece(core_dst, k, c),
+            send_sem=core_send.at[k, c], recv_sem=core_recv.at[k, c],
+            device_id=(z, sibling), device_id_type=MESH,
+        )
+
+    def first_copy(k, c):
+        return pltpu.make_async_remote_copy(
+            src_ref=piece(part, k, c), dst_ref=piece(first_dst, k, c),
+            send_sem=first_send.at[k, c], recv_sem=first_recv.at[k, c],
+            device_id=(z, first), device_id_type=MESH,
+        )
+
+    def second_copy(k, c):
+        return pltpu.make_async_remote_copy(
+            src_ref=piece(part, k, c), dst_ref=second_dst.at[pl.ds(c * per, per)],
+            send_sem=second_send.at[c], recv_sem=second_recv.at[c],
+            device_id=(z, second), device_id_type=MESH,
+        )
+
+    def goal(k):
+        b = block_at(k)
+        y_b, x_b = b // 2, b % 2
+        return x_b + core * (y_b - x_b), y_b + core * (x_b - y_b)
+
+    def multiply(k):
+        y_high, y_low = split(y_buf[block_at(k)])
+        y_hi[...] = y_high
+        y_lo[...] = y_low
+
+        @pl.loop(0, steps)
+        def _(s):
+            if k == 0:
+                pltpu.make_async_copy(panel.at[s], pf.at[s], panel_sem.at[s]).wait()
+                high, low = split(pf[s])
+                p_hi[s] = high
+                p_lo[s] = low
+            terms = dot3((p_hi[s], p_lo[s]), (y_hi[...], y_lo[...]))
+            half = terms.shape[1] // 2
+            part[k, s] = jnp.where(core == 0, terms[:, :half], terms[:, half:])
+            core_src[k, s] = jnp.where(core == 0, terms[:, half:], terms[:, :half])
+
+            @pl.when(s % per == per - 1)
+            def _():
+                core_copy(k, s // per).start()
+
+    def add_core(k):
+        f_b, _ = goal(k)
+
+        @pl.loop(0, chunks)
+        def _(c):
+            core_copy(k, c).wait_recv()
+            here = pl.ds(c * per, per)
+            part[k, here] = part[k, here] + core_dst[k, here]
+
+            @pl.when(f != f_b)
+            def _():
+                first_copy(k, c).start()
+
+    def add_first(k):
+        f_b, g_b = goal(k)
+
+        @pl.when(f == f_b)
+        def _():
+            @pl.loop(0, chunks)
+            def _(c):
+                first_copy(k, c).wait_recv()
+                here = pl.ds(c * per, per)
+                part[k, here] = part[k, here] + first_dst[k, here]
+
+                @pl.when(g != g_b)
+                def _():
+                    second_copy(k, c).start()
+
+    def chain_copy(which, ref, target, source):
+        here = ref.at[pl.ds(pl.multiple_of(source * rows, rows), rows)]
+        return pltpu.make_async_remote_copy(
+            src_ref=here, dst_ref=here, send_sem=chain_send.at[which, target],
+            recv_sem=chain_recv.at[which, source],
+            device_id=(target, col), device_id_type=MESH,
+        )
+
+    def spread(which, ref, down, finish=False):
+        for target in range(4):
+            @pl.when((z != target) if down else (z < target))
+            def _():
+                copy = chain_copy(which, ref, target, z)
+                copy.wait_send() if finish else copy.start()
+
+    def collect(which, ref, down):
+        for source in range(4):
+            @pl.when((z != source) if down else (z > source))
+            def _():
+                chain_copy(which, ref, (z + 1) % 4, source).wait_recv()
+
+    mine = pl.ds(pl.multiple_of(z * rows, rows), rows)
+
+    def finish_block(k):
+        @pl.when(block_at(k) == chip)
+        def _():
+            for c in range(chunks):
+                second_copy(k, c).wait_recv()
+                for s in range(c * per, (c + 1) * per):
+                    rest = rhs[s] - (part[k, s] + second_dst[s])
+                    if s == 0:
+                        r0_all[mine, :] = rest
+                        spread(0, r0_all, False)
+                    elif s == 1:
+                        r1[...] = rest
+                    else:
+                        pend_out[s - 2] = rest
+
+    own_sends()
+    for ref in (r0_all, s1_all):
+        for source in range(4):
+            @pl.when(source > z)
+            def _(ref=ref, source=source):
+                ref[source * rows:(source + 1) * rows, :] = jnp.zeros((rows, ref.shape[1]), F32)
+    own.wait()
+    multiply(0)
+    for copy in loads:
+        copy.wait()
+    add_core(0)
+
+    for k in range(1, 4):
+        if k == 2:
+            @pl.when(jnp.logical_not(middle))
+            def _():
+                arrived(block_at(2))
+        else:
+            arrived(block_at(k))
+            forward(block_at(k))
+        if k == 1:
+            @pl.when(middle)
+            def _():
+                arrived(block_at(2))
+                forward(block_at(2))
+        multiply(k)
+        add_first(k - 1)
+        add_core(k)
+        finish_block(k - 1)
+    add_first(3)
+    finish_block(3)
+
+    collect(0, r0_all, False)
+    first_solution = dot3(split(inv_v[0]), split(r0_all[...]))
+    y0_all[mine, :] = first_solution
+    spread(1, y0_all, True)
+    y_out[0] = first_solution
+    collect(1, y0_all, True)
+    s1_all[mine, :] = r1[...] - dot3(split(low_v[...]), split(y0_all[...]))
+    spread(2, s1_all, False)
+    collect(2, s1_all, False)
+    y_out[1] = dot3(split(inv_v[1]), split(s1_all[...]))
+
+    own_sends(True)
+    for k in range(1, 4):
+        forward(block_at(k), True)
+    for k in range(4):
+        f_b, g_b = goal(k)
+
+        @pl.loop(0, chunks)
+        def _(c):
+            core_copy(k, c).wait_send()
+
+            @pl.when(f != f_b)
+            def _():
+                first_copy(k, c).wait_send()
+
+            @pl.when((f == f_b) & (g != g_b))
+            def _():
+                second_copy(k, c).wait_send()
+
+    spread(0, r0_all, False, True)
+    spread(1, y0_all, True, True)
+    spread(2, s1_all, False, True)
+
+
+def fused(panel, prior_y, right_side, inv_blocks, lower_block):
+    steps, rows, depth = panel.shape
+    wide = prior_y.shape[1]
+    own = right_side.shape[2]
+    size = inv_blocks.shape[2]
+    chunks = 4
+    anywhere = pl.BlockSpec(memory_space=pl.ANY)
+    local = pl.BlockSpec(memory_space=pltpu.VMEM)
+    dma = pltpu.SemaphoreType.DMA
+    return pl.pallas_call(
+        kernel,
+        out_shape=(
+            jax.ShapeDtypeStruct((2, rows, own), F32),
+            jax.ShapeDtypeStruct((steps - 2, rows, own), F32),
+        ),
+        in_specs=[anywhere] * 5,
+        out_specs=(local, local),
+        scratch_shapes=[
+            pltpu.VMEM((steps, rows, depth), F32),
+            pltpu.VMEM((steps, rows, depth), BF16),
+            pltpu.VMEM((steps, rows, depth), BF16),
+            pltpu.VMEM((4, depth, wide), F32),
+            pltpu.VMEM((depth, wide), BF16),
+            pltpu.VMEM((depth, wide), BF16),
+            pltpu.VMEM((4, steps, rows, own), F32),
+            pltpu.VMEM((4, steps, rows, own), F32),
+            pltpu.VMEM((4, steps, rows, own), F32),
+            pltpu.VMEM((4, steps, rows, own), F32),
+            pltpu.VMEM((steps, rows, own), F32),
+            pltpu.VMEM((steps, rows, own), F32),
+            pltpu.VMEM((2, rows, size), F32),
+            pltpu.VMEM((rows, size), F32),
+            pltpu.VMEM((size, own), F32),
+            pltpu.VMEM((size, own), F32),
+            pltpu.VMEM((size, own), F32),
+            pltpu.VMEM((rows, own), F32),
+            dma((4,)),
+            dma((steps,)),
+            dma((6,)),
+            dma((4,)),
+            dma((4, chunks)),
+            dma((4, chunks)),
+            dma((4, chunks)),
+            dma((4, chunks)),
+            dma((chunks,)),
+            dma((chunks,)),
+            dma((3, 4)),
+            dma((3, 4)),
+        ],
+        compiler_params=pltpu.CompilerParams(
+            collective_id=0, has_side_effects=True, vmem_limit_bytes=60 * 1024 * 1024
+        ),
+    )(panel, prior_y, right_side, inv_blocks, lower_block)
+
+
+def general(panel, prior_y, right_side, inv_blocks, lower_block):
     highest = lax.Precision.HIGHEST
     terms = jnp.einsum(
         "sip,pm->sim",
@@ -38,8 +376,9 @@
         P(None, "row", None),
         P("row", None),
     )
+    four_by_eight = mesh.shape["row"] == 4 and mesh.shape["col"] == 8
     return jax.shard_map(
-        body,
+        fused if four_by_eight else general,
         mesh=mesh,
         in_specs=placed,
         out_specs=(P(None, "row", "col"), P(None, "row", "col")),

time: 257 us -> 146 us (0.57)
  the two profiles are of different devices: /device:TPU:0 before, /device:TPU:31 now
where the time goes in v1:
time: 146 us; the launch traced here: 145 us
  Pallas kernels  141 us (97%)
  local copies, waits for them, and re-layouts  3.73 us (3%)
    pallas_call x1, Pallas kernels, fused(): pl.pallas_call(kernel, out_shape=(jax.ShapeDtypeStruct((2, rows, own), F3...  141 us
    unnamed x2, local copies, waits for them, and re-layouts  3.73 us

profile of v1, /device:TPU:31, one launch (start us, length us, event | category | flops | bytes accessed | tf_op | source)
XLA Modules:
  0.0 145.4 jit_solution(14975528334354163038)
XLA Ops:
  0.6 141.0 %shard_map.68 = (f32[2,256,128]{2,1,0:T(8,128)}, f32[6,256,128]{2,1,0:T(8,128)}) custom-call(f32[8,256,1024]{2,1,0:T(8,128)} %panel.1, f32[1024,256]{1,0:T(8,128)} %prior.1, f32[8,256,128]{2,1,0:T(8,128)} %right.1, f32[2,256,1024]{2,1,0:T(8,128)} %inv.1, f32[256,1024]{1,0:T(8,128)} %lower.1), custom_call_target="tpu_custom_call" | custom-call | tf_op jit(solution)/shard_map/pallas_call | solution.py:299
  141.6 1.7 %copy.9 = f32[2,256,128]{2,1,0:T(8,128)} copy(f32[2,256,128]{2,1,0:T(8,128)} %get-tuple-element.4) | data formatting | bytes 524288
  143.3 2.1 %copy.10 = f32[6,256,128]{2,1,0:T(8,128)} copy(f32[6,256,128]{2,1,0:T(8,128)} %get-tuple-element.5) | data formatting | bytes 1572864

commit v2 on v1

--- a/solution.py
+++ b/solution.py
@@ -26,12 +26,13 @@
 
 def kernel(
     panel, prior, right, inv, lower, y_out, pend_out,
-    pf, p_hi, p_lo, y_buf, y_hi, y_lo, core_src, core_dst, part, first_dst, second_dst,
+    pf, p_hi, p_lo, y_buf, y_cat, core_src, core_dst, part, first_dst, second_dst,
     rhs, inv_v, low_v, r0_all, y0_all, s1_all, r1,
-    load_sem, panel_sem, y_send, y_recv, core_send, core_recv, first_send, first_recv,
+    load_sem, own_sem, panel_sem, y_send, y_recv, core_send, core_recv, first_send, first_recv,
     second_send, second_recv, chain_send, chain_recv,
 ):
     steps, rows, depth = pf.shape
+    wide = rhs.shape[2]
     chunks = core_send.shape[1]
     per = steps // chunks
     z = lax.axis_index("row")
@@ -40,10 +41,6 @@
     chip = col // 2
     sibling = col + 1 - 2 * core
     x_near, y_near = col + 2 - 4 * x, col + 4 - 8 * y
-    first = x_near + core * (y_near - x_near)
-    second = y_near + core * (x_near - y_near)
-    f = x + core * (y - x)
-    g = y + core * (x - y)
     middle = (z == 1) | (z == 2)
     upper = z // 2
     z_fold = z + upper * (3 - 2 * z)
@@ -52,17 +49,22 @@
         b = (z_fold, 1 - z_fold, 2, 3)[k]
         return b + upper * (3 - 2 * b)
 
-    own = pltpu.make_async_copy(prior, y_buf.at[z], load_sem.at[0])
-    own.start()
-    panel_copies = [
-        pltpu.make_async_copy(panel.at[s], pf.at[s], panel_sem.at[s]) for s in range(steps)
-    ]
-    for copy in panel_copies:
+    def half_of(h):
+        return prior.at[:, h * wide:(h + 1) * wide]
+
+    own = [pltpu.make_async_copy(half_of(h), y_buf.at[z, h], own_sem.at[h]) for h in range(2)]
+    for copy in own:
         copy.start()
+
+    def panel_copy(s):
+        return pltpu.make_async_copy(panel.at[s], pf.at[s], panel_sem.at[s])
+
+    for s in range(steps):
+        panel_copy(s).start()
     loads = [
-        pltpu.make_async_copy(right, rhs, load_sem.at[1]),
-        pltpu.make_async_copy(inv, inv_v, load_sem.at[2]),
-        pltpu.make_async_copy(lower, low_v, load_sem.at[3]),
+        pltpu.make_async_copy(right, rhs, load_sem.at[0]),
+        pltpu.make_async_copy(inv, inv_v, load_sem.at[1]),
+        pltpu.make_async_copy(lower, low_v, load_sem.at[2]),
     ]
     for copy in loads:
         copy.start()
@@ -74,39 +76,42 @@
         pl.semaphore_signal(barrier, inc=1, device_id=((z + j) % 4, col), device_id_type=MESH)
     pl.semaphore_wait(barrier, 6)
 
-    def along_z(src, b, target, sem):
+    def along_z(src, b, h, target, sem):
         return pltpu.make_async_remote_copy(
-            src_ref=src, dst_ref=y_buf.at[b], send_sem=y_send.at[sem], recv_sem=y_recv.at[b],
-            device_id=(target, col), device_id_type=MESH,
+            src_ref=src, dst_ref=y_buf.at[b, h], send_sem=y_send.at[sem, h],
+            recv_sem=y_recv.at[b, h], device_id=(target, col), device_id_type=MESH,
         )
 
-    def forward(b, finish=False):
+    def forward(b, h, finish=False):
         @pl.when((b < z) & (z < 3))
         def _():
-            copy = along_z(y_buf.at[b], b, z + 1, 2 + b)
+            copy = along_z(y_buf.at[b, h], b, h, z + 1, 2 + b)
             copy.wait_send() if finish else copy.start()
 
         @pl.when((b > z) & (z > 0))
         def _():
-            copy = along_z(y_buf.at[b], b, z - 1, 2 + b)
+            copy = along_z(y_buf.at[b, h], b, h, z - 1, 2 + b)
             copy.wait_send() if finish else copy.start()
 
-    def own_sends(finish=False):
+    def own_sends(h, finish=False):
         @pl.when(z < 3)
         def _():
-            copy = along_z(prior, z, z + 1, 0)
+            copy = along_z(half_of(h), z, h, z + 1, 0)
             copy.wait_send() if finish else copy.start()
 
         @pl.when(z > 0)
         def _():
-            copy = along_z(prior, z, z - 1, 1)
+            copy = along_z(half_of(h), z, h, z - 1, 1)
             copy.wait_send() if finish else copy.start()
 
-    def arrived(b):
-        along_z(y_buf.at[b], b, (z + 1) % 4, 0).wait_recv()
+    def arrived(b, h):
+        along_z(y_buf.at[b, h], b, h, (z + 1) % 4, 0).wait_recv()
 
     def piece(ref, k, c):
         return ref.at[k, pl.ds(c * per, per)]
+
+    def order(c, along_x, along_y):
+        return along_x + (c % 2) * (along_y - along_x)
 
     def core_copy(k, c):
         return pltpu.make_async_remote_copy(
@@ -119,67 +124,75 @@
         return pltpu.make_async_remote_copy(
             src_ref=piece(part, k, c), dst_ref=piece(first_dst, k, c),
             send_sem=first_send.at[k, c], recv_sem=first_recv.at[k, c],
-            device_id=(z, first), device_id_type=MESH,
+            device_id=(z, order(c, x_near, y_near)), device_id_type=MESH,
         )
 
     def second_copy(k, c):
         return pltpu.make_async_remote_copy(
             src_ref=piece(part, k, c), dst_ref=second_dst.at[pl.ds(c * per, per)],
             send_sem=second_send.at[c], recv_sem=second_recv.at[c],
-            device_id=(z, second), device_id_type=MESH,
+            device_id=(z, order(c, y_near, x_near)), device_id_type=MESH,
         )
 
-    def goal(k):
+    def first_away(k, c):
         b = block_at(k)
-        y_b, x_b = b // 2, b % 2
-        return x_b + core * (y_b - x_b), y_b + core * (x_b - y_b)
-
-    def multiply(k):
-        y_high, y_low = split(y_buf[block_at(k)])
-        y_hi[...] = y_high
-        y_lo[...] = y_low
-
-        @pl.loop(0, steps)
-        def _(s):
-            if k == 0:
-                pltpu.make_async_copy(panel.at[s], pf.at[s], panel_sem.at[s]).wait()
-                high, low = split(pf[s])
-                p_hi[s] = high
-                p_lo[s] = low
-            terms = dot3((p_hi[s], p_lo[s]), (y_hi[...], y_lo[...]))
-            half = terms.shape[1] // 2
-            part[k, s] = jnp.where(core == 0, terms[:, :half], terms[:, half:])
-            core_src[k, s] = jnp.where(core == 0, terms[:, half:], terms[:, :half])
-
-            @pl.when(s % per == per - 1)
-            def _():
-                core_copy(k, s // per).start()
+        return order(c, x, y) != order(c, b % 2, b // 2)
+
+    def second_away(k, c):
+        b = block_at(k)
+        return order(c, y, x) != order(c, b // 2, b % 2)
+
+    def multiply(k, h):
+        high, low = split(y_buf[block_at(k), h])
+        y_cat[:, :wide] = high
+        y_cat[:, wide:] = low
+
+        @pl.loop(0, chunks)
+        def _(c):
+            here = pl.ds(c * per, per)
+            if k == 0 and h == 0:
+                for i in range(per):
+                    s = c * per + i
+                    panel_copy(s).wait()
+                    high, low = split(pf[s])
+                    p_hi[s] = high
+                    p_lo[s] = low
+            left = p_hi[here].reshape(per * rows, depth)
+            both = jnp.dot(left, y_cat[...], preferred_element_type=F32)
+            left = p_lo[here].reshape(per * rows, depth)
+            rest = jnp.dot(left, y_cat[:, :wide], preferred_element_type=F32)
+            terms = (both[:, :wide] + (both[:, wide:] + rest)).reshape(per, rows, wide)
+
+            @pl.when(core == h)
+            def _():
+                part[k, here] = terms
+
+            @pl.when(core != h)
+            def _():
+                core_src[k, here] = terms
+                core_copy(k, c).start()
 
     def add_core(k):
-        f_b, _ = goal(k)
-
         @pl.loop(0, chunks)
         def _(c):
             core_copy(k, c).wait_recv()
             here = pl.ds(c * per, per)
             part[k, here] = part[k, here] + core_dst[k, here]
 
-            @pl.when(f != f_b)
+            @pl.when(first_away(k, c))
             def _():
                 first_copy(k, c).start()
 
-    def add_first(k):
-        f_b, g_b = goal(k)
-
-        @pl.when(f == f_b)
-        def _():
-            @pl.loop(0, chunks)
-            def _(c):
+    def add_first(k, low, high):
+        @pl.loop(low, high)
+        def _(c):
+            @pl.when(jnp.logical_not(first_away(k, c)))
+            def _():
                 first_copy(k, c).wait_recv()
                 here = pl.ds(c * per, per)
                 part[k, here] = part[k, here] + first_dst[k, here]
 
-                @pl.when(g != g_b)
+                @pl.when(second_away(k, c))
                 def _():
                     second_copy(k, c).start()
 
@@ -206,10 +219,10 @@
 
     mine = pl.ds(pl.multiple_of(z * rows, rows), rows)
 
-    def finish_block(k):
+    def finish_block(k, low, high):
         @pl.when(block_at(k) == chip)
         def _():
-            for c in range(chunks):
+            for c in range(low, high):
                 second_copy(k, c).wait_recv()
                 for s in range(c * per, (c + 1) * per):
                     rest = rhs[s] - (part[k, s] + second_dst[s])
@@ -221,64 +234,82 @@
                     else:
                         pend_out[s - 2] = rest
 
-    own_sends()
+    for h in range(2):
+        own_sends(h)
     for ref in (r0_all, s1_all):
         for source in range(4):
             @pl.when(source > z)
             def _(ref=ref, source=source):
-                ref[source * rows:(source + 1) * rows, :] = jnp.zeros((rows, ref.shape[1]), F32)
-    own.wait()
-    multiply(0)
-    for copy in loads:
-        copy.wait()
-    add_core(0)
-
-    for k in range(1, 4):
-        if k == 2:
-            @pl.when(jnp.logical_not(middle))
-            def _():
-                arrived(block_at(2))
-        else:
-            arrived(block_at(k))
-            forward(block_at(k))
-        if k == 1:
-            @pl.when(middle)
-            def _():
-                arrived(block_at(2))
-                forward(block_at(2))
-        multiply(k)
-        add_first(k - 1)
-        add_core(k)
-        finish_block(k - 1)
-    add_first(3)
-    finish_block(3)
+                ref[source * rows:(source + 1) * rows, :] = jnp.zeros((rows, wide), F32)
+
+    for k in range(4):
+        for h in range(2):
+            if k == 0:
+                own[h].wait()
+            elif k == 2:
+                @pl.when(jnp.logical_not(middle))
+                def _():
+                    arrived(block_at(2), h)
+            else:
+                arrived(block_at(k), h)
+                forward(block_at(k), h)
+            if k == 1:
+                @pl.when(middle)
+                def _():
+                    arrived(block_at(2), h)
+                    forward(block_at(2), h)
+            multiply(k, h)
+            if k == 0 and h == 0:
+                for copy in loads:
+                    copy.wait()
+
+            @pl.when(core == h)
+            def _():
+                add_core(k)
+                if k > 0:
+                    finish_block(k - 1, 0, chunks)
+
+            if h == 1 or k > 0:
+                @pl.when(core != h)
+                def _():
+                    add_first(k if h == 1 else k - 1, 0, chunks)
+
+    @pl.when(core == 1)
+    def _():
+        add_first(3, 0, 1)
+
+    finish_block(3, 0, 1)
+
+    @pl.when(core == 1)
+    def _():
+        add_first(3, 1, chunks)
 
     collect(0, r0_all, False)
     first_solution = dot3(split(inv_v[0]), split(r0_all[...]))
     y0_all[mine, :] = first_solution
     spread(1, y0_all, True)
     y_out[0] = first_solution
+    finish_block(3, 1, chunks)
     collect(1, y0_all, True)
     s1_all[mine, :] = r1[...] - dot3(split(low_v[...]), split(y0_all[...]))
     spread(2, s1_all, False)
     collect(2, s1_all, False)
     y_out[1] = dot3(split(inv_v[1]), split(s1_all[...]))
 
-    own_sends(True)
-    for k in range(1, 4):
-        forward(block_at(k), True)
+    for h in range(2):
+        own_sends(h, True)
+        for k in range(1, 4):
+            forward(block_at(k), h, True)
     for k in range(4):
-        f_b, g_b = goal(k)
-
         @pl.loop(0, chunks)
         def _(c):
             core_copy(k, c).wait_send()
 
-            @pl.when(f != f_b)
+            @pl.when(first_away(k, c))
             def _():
                 first_copy(k, c).wait_send()
 
-            @pl.when((f == f_b) & (g != g_b))
+            @pl.when(jnp.logical_not(first_away(k, c)) & second_away(k, c))
             def _():
                 second_copy(k, c).wait_send()
 
@@ -289,7 +320,6 @@
 
 def fused(panel, prior_y, right_side, inv_blocks, lower_block):
     steps, rows, depth = panel.shape
-    wide = prior_y.shape[1]
     own = right_side.shape[2]
     size = inv_blocks.shape[2]
     chunks = 4
@@ -308,9 +338,8 @@
             pltpu.VMEM((steps, rows, depth), F32),
             pltpu.VMEM((steps, rows, depth), BF16),
             pltpu.VMEM((steps, rows, depth), BF16),
-            pltpu.VMEM((4, depth, wide), F32),
-            pltpu.VMEM((depth, wide), BF16),
-            pltpu.VMEM((depth, wide), BF16),
+            pltpu.VMEM((4, 2, depth, own), F32),
+            pltpu.VMEM((depth, 2 * own), BF16),
             pltpu.VMEM((4, steps, rows, own), F32),
             pltpu.VMEM((4, steps, rows, own), F32),
             pltpu.VMEM((4, steps, rows, own), F32),
@@ -323,10 +352,11 @@
             pltpu.VMEM((size, own), F32),
             pltpu.VMEM((size, own), F32),
             pltpu.VMEM((rows, own), F32),
-            dma((4,)),
+            dma((3,)),
+            dma((2,)),
             dma((steps,)),
-            dma((6,)),
-            dma((4,)),
+            dma((6, 2)),
+            dma((4, 2)),
             dma((4, chunks)),
             dma((4, chunks)),
             dma((4, chunks)),

time: 146 us -> 124 us (0.85)
  Pallas kernels: 141 us -> 120 us
    pallas_call x1, Pallas kernels: 141 us -> 120 us  [fused(): pl.pallas_call(kernel, out_shape=(jax.ShapeDtypeStruct((2, rows, own), F3...]
where the time goes in v2:
time: 124 us
  Pallas kernels  120 us (97%)
  local copies, waits for them, and re-layouts  3.73 us (3%)
    pallas_call x1, Pallas kernels, fused(): pl.pallas_call(kernel, out_shape=(jax.ShapeDtypeStruct((2, rows, own), F3...  120 us
    unnamed x2, local copies, waits for them, and re-layouts  3.73 us

profile of v2, /device:TPU:31, one launch (start us, length us, event | category | flops | bytes accessed | tf_op | source)
XLA Modules:
  0.0 124.1 jit_solution(10671962482304515374)
XLA Ops:
  0.6 119.7 %shard_map.68 = (f32[2,256,128]{2,1,0:T(8,128)}, f32[6,256,128]{2,1,0:T(8,128)}) custom-call(f32[8,256,1024]{2,1,0:T(8,128)} %panel.1, f32[1024,256]{1,0:T(8,128)} %prior.1, f32[8,256,128]{2,1,0:T(8,128)} %right.1, f32[2,256,1024]{2,1,0:T(8,128)} %inv.1, f32[256,1024]{1,0:T(8,128)} %lower.1), custom_call_target="tpu_custom_call" | custom-call | tf_op jit(solution)/shard_map/pallas_call | solution.py:329
  120.4 1.7 %copy.9 = f32[2,256,128]{2,1,0:T(8,128)} copy(f32[2,256,128]{2,1,0:T(8,128)} %get-tuple-element.4) | data formatting | bytes 524288
  122.0 2.1 %copy.10 = f32[6,256,128]{2,1,0:T(8,128)} copy(f32[6,256,128]{2,1,0:T(8,128)} %get-tuple-element.5) | data formatting | bytes 1572864

commit v3 on v2

--- a/solution.py
+++ b/solution.py
@@ -27,7 +27,7 @@
 def kernel(
     panel, prior, right, inv, lower, y_out, pend_out,
     pf, p_hi, p_lo, y_buf, y_cat, core_src, core_dst, part, first_dst, second_dst,
-    rhs, inv_v, low_v, r0_all, y0_all, s1_all, r1,
+    rhs, inv_v, low_v, m_hi, m_lo, r0_all, y0_all, s1_all, r1,
     load_sem, own_sem, panel_sem, y_send, y_recv, core_send, core_recv, first_send, first_recv,
     second_send, second_recv, chain_send, chain_recv,
 ):
@@ -35,6 +35,7 @@
     wide = rhs.shape[2]
     chunks = core_send.shape[1]
     per = steps // chunks
+    lag = 2
     z = lax.axis_index("row")
     col = lax.axis_index("col")
     y, x, core = col // 4, (col // 2) % 2, col % 2
@@ -141,6 +142,15 @@
     def second_away(k, c):
         b = block_at(k)
         return order(c, y, x) != order(c, b // 2, b % 2)
+
+    def add_core(k, c):
+        core_copy(k, c).wait_recv()
+        here = pl.ds(c * per, per)
+        part[k, here] = part[k, here] + core_dst[k, here]
+
+        @pl.when(first_away(k, c))
+        def _():
+            first_copy(k, c).start()
 
     def multiply(k, h):
         high, low = split(y_buf[block_at(k), h])
@@ -167,21 +177,14 @@
             def _():
                 part[k, here] = terms
 
+                @pl.when(c >= lag)
+                def _():
+                    add_core(k, c - lag)
+
             @pl.when(core != h)
             def _():
                 core_src[k, here] = terms
                 core_copy(k, c).start()
-
-    def add_core(k):
-        @pl.loop(0, chunks)
-        def _(c):
-            core_copy(k, c).wait_recv()
-            here = pl.ds(c * per, per)
-            part[k, here] = part[k, here] + core_dst[k, here]
-
-            @pl.when(first_away(k, c))
-            def _():
-                first_copy(k, c).start()
 
     def add_first(k, low, high):
         @pl.loop(low, high)
@@ -234,8 +237,8 @@
                     else:
                         pend_out[s - 2] = rest
 
-    for h in range(2):
-        own_sends(h)
+    own_sends(0)
+    own_sends(1)
     for ref in (r0_all, s1_all):
         for source in range(4):
             @pl.when(source > z)
@@ -262,10 +265,16 @@
             if k == 0 and h == 0:
                 for copy in loads:
                     copy.wait()
+            if k == 0 and h == 1:
+                for i, ref in enumerate((inv_v.at[0], low_v, inv_v.at[1])):
+                    high, low = split(ref[...])
+                    m_hi[i] = high
+                    m_lo[i] = low
 
             @pl.when(core == h)
             def _():
-                add_core(k)
+                for c in range(chunks - lag, chunks):
+                    add_core(k, c)
                 if k > 0:
                     finish_block(k - 1, 0, chunks)
 
@@ -285,21 +294,22 @@
         add_first(3, 1, chunks)
 
     collect(0, r0_all, False)
-    first_solution = dot3(split(inv_v[0]), split(r0_all[...]))
+    first_solution = dot3((m_hi[0], m_lo[0]), split(r0_all[...]))
     y0_all[mine, :] = first_solution
     spread(1, y0_all, True)
     y_out[0] = first_solution
     finish_block(3, 1, chunks)
     collect(1, y0_all, True)
-    s1_all[mine, :] = r1[...] - dot3(split(low_v[...]), split(y0_all[...]))
+    s1_all[mine, :] = r1[...] - dot3((m_hi[1], m_lo[1]), split(y0_all[...]))
     spread(2, s1_all, False)
     collect(2, s1_all, False)
-    y_out[1] = dot3(split(inv_v[1]), split(s1_all[...]))
+    y_out[1] = dot3((m_hi[2], m_lo[2]), split(s1_all[...]))
 
     for h in range(2):
         own_sends(h, True)
         for k in range(1, 4):
             forward(block_at(k), h, True)
+
     for k in range(4):
         @pl.loop(0, chunks)
         def _(c):
@@ -322,7 +332,7 @@
     steps, rows, depth = panel.shape
     own = right_side.shape[2]
     size = inv_blocks.shape[2]
-    chunks = 4
+    chunks = 8
     anywhere = pl.BlockSpec(memory_space=pl.ANY)
     local = pl.BlockSpec(memory_space=pltpu.VMEM)
     dma = pltpu.SemaphoreType.DMA
@@ -348,6 +358,8 @@
             pltpu.VMEM((steps, rows, own), F32),
             pltpu.VMEM((2, rows, size), F32),
             pltpu.VMEM((rows, size), F32),
+            pltpu.VMEM((3, rows, size), BF16),
+            pltpu.VMEM((3, rows, size), BF16),
             pltpu.VMEM((size, own), F32),
             pltpu.VMEM((size, own), F32),
             pltpu.VMEM((size, own), F32),

time: 124 us -> 121 us (0.976)
  Pallas kernels: 120 us -> 116 us
    pallas_call x1, Pallas kernels: 120 us -> 116 us  [fused(): pl.pallas_call(kernel, out_shape=(jax.ShapeDtypeStruct((2, rows, own), F3...]
where the time goes in v3:
time: 121 us
  Pallas kernels  116 us (96%)
  local copies, waits for them, and re-layouts  3.73 us (3%)
    pallas_call x1, Pallas kernels, fused(): pl.pallas_call(kernel, out_shape=(jax.ShapeDtypeStruct((2, rows, own), F3...  116 us
    unnamed x2, local copies, waits for them, and re-layouts  3.73 us

profile of v3, /device:TPU:31, one launch (start us, length us, event | category | flops | bytes accessed | tf_op | source)
XLA Modules:
  0.0 120.9 jit_solution(14654456560781218658)
XLA Ops:
  0.6 116.5 %shard_map.68 = (f32[2,256,128]{2,1,0:T(8,128)}, f32[6,256,128]{2,1,0:T(8,128)}) custom-call(f32[8,256,1024]{2,1,0:T(8,128)} %panel.1, f32[1024,256]{1,0:T(8,128)} %prior.1, f32[8,256,128]{2,1,0:T(8,128)} %right.1, f32[2,256,1024]{2,1,0:T(8,128)} %inv.1, f32[256,1024]{1,0:T(8,128)} %lower.1), custom_call_target="tpu_custom_call" | custom-call | tf_op jit(solution)/shard_map/pallas_call | solution.py:339
  117.1 1.7 %copy.9 = f32[2,256,128]{2,1,0:T(8,128)} copy(f32[2,256,128]{2,1,0:T(8,128)} %get-tuple-element.4) | data formatting | bytes 524288
  118.8 2.1 %copy.10 = f32[6,256,128]{2,1,0:T(8,128)} copy(f32[6,256,128]{2,1,0:T(8,128)} %get-tuple-element.5) | data formatting | bytes 1572864
